TPU v7x, 32 devices: a whole 2x2x4 slice. The times are simulated.
32 devices in a mesh: sec: 4 (over y, x), ctx: 2 (over core), ch: 4 (over z).
Axes of the slice: x: 2, y: 2, z: 4, core: 2. Of those that a mesh axis runs over, the one named last changes fastest.
Arguments:
- inputs: bfloat16 [256, 4096], P('ctx', ('ch', 'sec')), may hold values from -2500 to 2500, as said below
- query_fields: bfloat16 [4, 256, 4096], P('sec', 'ctx', 'ch'), may hold values from -3 to 3
- key_fields: bfloat16 [4, 256, 4096], P('sec', 'ctx', 'ch'), may hold values from -4 to 4
- norm_gain: float32 [4096], P('ch'), may hold values from 0.1 to 1.9
- short_taps: float32 [2, 7, 4096], P(None, None, 'ch'), may hold values from -2 to 2
- medium_taps: float32 [128, 4096], P(None, 'ch'), may hold values from -0.5 to 0.5
- pole_rates: float32 [8, 4096], P(None, 'ch'), as said below
- pole_residues: float32 [8, 4096], P(None, 'ch'), may hold values from -2 to 2
- direct_term: float32 [4096], P('ch'), may hold values from -3 to 3
Outputs:
- mixed_stream: bfloat16 [256, 4096], P('ctx', ('ch', 'sec'))
Inputs may be any that keep to these rules, and one draw needn't show every extreme that they name: `inputs`: scaled real values. `pole_rates`: Positive, from 0.2 / 256 to 1 / 30.
All inputs are finite; a program needn't handle non-finite values.
Results may differ from a plain program's by a relative error of at most 0.013.
Values may be sent and summed in bfloat16 or wider, within the bound.
A program may use at most 64 MiB of HBM per device.

v0:
```python
import jax
import jax.numpy as jnp
from jax import lax
from jax.sharding import PartitionSpec as P

D = 4096


norm_eps = 1e-06


def prefix_2(value, axis, join, neutral):
    count, mine = (lax.axis_size(axis), lax.axis_index(axis))
    pieces = jax.tree.map(lambda part: lax.all_gather(part, axis), value)
    total = jax.tree.map(
        lambda part, zero: jnp.full_like(part, 0) + jnp.asarray(zero, part.dtype), value, neutral
    )

    def hop(position, total):
        longer = join(total, jax.tree.map(lambda part: part[position], pieces))
        return jax.tree.map(lambda new, old: jnp.where(position < mine, new, old), longer, total)

    return lax.fori_loop(0, count - 1, hop, total)


def passed_along(value, axis, steps):
    count = lax.axis_size(axis)
    first, last = (max(0, -steps), min(count, count - steps))
    return lax.ppermute(value, axis, [(source, source + steps) for source in range(first, last)])


def batched_depthwise(padded, flipped_taps):
    channels = padded.shape[2]
    return lax.conv_general_dilated(
        padded,
        flipped_taps[:, None, :],
        window_strides=(1,),
        padding="VALID",
        dimension_numbers=("NWC", "WIO", "NWC"),
        feature_group_count=channels,
        precision=lax.Precision.HIGHEST,
    )


def finite_filter(gated, before, filter_taps):
    span = filter_taps.shape[0]
    joined = jnp.concatenate([before[before.shape[0] - (span - 1) :], gated], axis=0)
    return batched_depthwise(joined[None], jnp.flip(filter_taps, 0))[0]


def piece_length(length):
    if length % 128 == 0:
        return 128
    return length


def modal_sum(weights, rates, length):
    offsets = jnp.arange(length, dtype=jnp.float32)
    return jnp.sum(weights[None] * jnp.exp(-rates[None] * offsets[:, None, None]), axis=1)


def piece_ends(gated, rates):
    length = gated.shape[0]
    width = piece_length(length)
    pieces = gated.reshape(length // width, width, gated.shape[1])
    row_ages = jnp.arange(width - 1, -1, -1, dtype=jnp.float32)
    table = jnp.exp(-rates[None] * row_ages[:, None, None])
    ends = jnp.einsum("imc,bic->bmc", table, pieces, precision=lax.Precision.HIGHEST)
    return (pieces, ends)


def long_filter(long_data, rates, residues, direct):
    pieces, ends, incoming = long_data
    count, width, channels = pieces.shape
    weights = residues * jnp.sqrt(-jnp.expm1(-2.0 * rates))
    kernel = modal_sum(weights, rates, width)
    padded = jnp.concatenate([jnp.zeros((count, width - 1, channels), jnp.float32), pieces], axis=1)
    within = batched_depthwise(padded, jnp.flip(kernel, 0))
    span_decay = jnp.exp(-rates * width)
    entering = []
    state = incoming
    for index in range(count):
        entering.append(state)
        state = span_decay * state + ends[index]
    entering = jnp.stack(entering)
    offsets = jnp.arange(1, width + 1, dtype=jnp.float32)
    carry_table = weights[None] * jnp.exp(-rates[None] * offsets[:, None, None])
    carried = jnp.einsum("kmc,bmc->bkc", carry_table, entering, precision=lax.Precision.HIGHEST)
    gated = pieces.reshape(count * width, channels)
    return (within + carried).reshape(count * width, channels) + direct[None] * gated


def combine(earlier, later):
    return (earlier[0] * later[1] + later[0], earlier[1] * later[1])


def carry_in(ends, rates, width, length):
    span_decay = jnp.exp(-rates * width)
    total = jnp.zeros_like(ends[0])
    for index in range(ends.shape[0]):
        total = span_decay * total + ends[index]
    powers = jnp.exp(-rates * length)
    empty = (jnp.zeros_like(total), jnp.ones_like(powers))
    prefix = prefix_2((total, powers), "ctx", combine, empty)
    return prefix[0]


def long_inputs(gated, rates):
    pieces, ends = piece_ends(gated, rates)
    incoming = carry_in(ends, rates, pieces.shape[1], gated.shape[0])
    return (pieces, ends, incoming)


def previous_rows(gated, count):
    return passed_along(gated[gated.shape[0] - count :], "ctx", 1)


def block_params(
    block_index, block_width, short_taps, medium_taps, pole_rates, pole_residues, direct_term
):

    def channel_cut(tables):
        return lax.dynamic_slice_in_dim(
            tables, block_index * block_width, block_width, tables.ndim - 1
        )

    return (
        channel_cut(short_taps),
        channel_cut(medium_taps),
        channel_cut(pole_rates),
        channel_cut(pole_residues),
        channel_cut(direct_term),
    )


def section_filter(kind, gated, before, long_data, params):
    short_pair, medium_block, rate_block, residue_block, direct_block = params
    if kind == 0:
        return finite_filter(gated, before, short_pair[0])
    if kind == 1:
        return finite_filter(gated, before, medium_block)
    if kind == 2:
        return long_filter(long_data, rate_block, residue_block, direct_block)
    return finite_filter(gated, before, short_pair[1])


def gate_update(current, query_block, filtered):
    return (current.astype(jnp.float32) + query_block.astype(jnp.float32) * filtered).astype(
        jnp.bfloat16
    )


def shards(
    inputs,
    query_fields,
    key_fields,
    norm_gain,
    short_taps,
    medium_taps,
    pole_rates,
    pole_residues,
    direct_term,
):
    sections = lax.axis_size("sec")
    segment_index = lax.axis_index("sec")
    block_width = inputs.shape[1]
    squares = jnp.sum(jnp.square(inputs.astype(jnp.float32)), axis=1)
    summed = lax.psum(squares, ("sec", "ch"))
    inverse_rms = lax.rsqrt(summed / D + norm_eps)
    gain_block = lax.dynamic_slice_in_dim(norm_gain, segment_index * block_width, block_width, 0)
    stream = (inputs.astype(jnp.float32) * inverse_rms[:, None] * gain_block[None]).astype(
        jnp.bfloat16
    )
    query_all, key_all = (
        lax.all_to_all(query_fields, "sec", split_axis=2, concat_axis=0, tiled=True),
        lax.all_to_all(key_fields, "sec", split_axis=2, concat_axis=0, tiled=True),
    )
    params = block_params(
        segment_index, block_width, short_taps, medium_taps, pole_rates, pole_residues, direct_term
    )
    for section in range(sections):
        gated = key_all[section].astype(jnp.float32) * stream.astype(jnp.float32)
        if section == 2:
            long_data = long_inputs(gated, params[2])
            filtered = section_filter(2, gated, None, long_data, params)
        else:
            if section == 1:
                span = params[1].shape[0]
            else:
                span = params[0].shape[1]
            before = previous_rows(gated, span - 1)
            filtered = section_filter(section, gated, before, None, params)
        stream = gate_update(stream, query_all[section], filtered)
    return stream


def solution(mesh):
    in_specs = (
        P("ctx", ("ch", "sec")),
        P("sec", "ctx", "ch"),
        P("sec", "ctx", "ch"),
        P("ch"),
        P(None, None, "ch"),
        P(None, "ch"),
        P(None, "ch"),
        P(None, "ch"),
        P("ch"),
    )
    out_specs = P("ctx", ("ch", "sec"))
    return jax.shard_map(shards, mesh=mesh, in_specs=in_specs, out_specs=out_specs, check_vma=False)
```

profile of v0, /device:TPU:1, one launch (start us, length us, event | category | flops | bytes accessed | tf_op | source)
XLA Modules:
  0.0 83.2 jit_solution(7332864765641143024)
XLA Ops:
  0.0 0.0 copy-start
  0.0 1.3 %copy.51 = bf16[1,128,1024]{1,0,2:T(2,128)(2,1)S(1)} copy(bf16[1,128,1024]{2,1,0:T(8,128)(2,1)} %param.11) | data formatting | bytes 524288 | tf_op args[2]
  1.3 0.5 broadcast.82
  1.8 2.2 %reduce.4 = bf16[1024,128]{1,0:T(8,128)(2,1)S(1)} reduce(bf16[1024,1,128]{2,1,0:T(2,128)(2,1)S(1)} %bitcast.133, bf16[]{:T(256)} %broadcast.82), dimensions={1}, to_apply=%bitcast.118.reduce_sub_computation | reduce | bytes 524290
  4.1 0.8 reshape.106
  4.8 0.0 copy-start.1
  4.8 0.0 copy-start.2
  4.8 4.4 %all-to-all-start.1 = ((bf16[4,2,16384]{2,1,0:T(2,128)(2,1)}), bf16[4,2,16384]{2,1,0:T(2,128)(2,1)S(1)}, u32[]{:S(2)}, u32[]{:S(2)}) async-start(bf16[4,2,16384]{2,1,0:T(2,128)(2,1)} %reshape.106), calls=%async_computation.1 | async-start | bytes 524288 | tf_op jit(solution)/shard_map/all_to_all | solution.py:176
  9.2 0.0 copy-done.1
  9.2 0.1 fusion.8
  9.3 35.2 %psum.7 = f32[128]{0:T(128)S(1)} all-reduce(f32[128]{0:T(128)S(1)} %fusion.8), channel_id=1, replica_groups=mesh['sec'=4,'ctx'=2,'ch'=4] {'sec','ch'}, use_global_device_ids=true, to_apply=%region_1.0 | all-reduce | flops 128 | bytes 1024 | tf_op jit(solution)/shard_map/psum | solution.py:168
  44.5 0.0 copy-done.2
  44.5 0.4 copy.49
  44.9 2.2 %reduce.5 = bf16[1024,128]{1,0:T(8,128)(2,1)S(1)} reduce(bf16[1024,1,128]{2,1,0:T(2,128)(2,1)S(1)} %bitcast.134, bf16[]{:T(256)} %broadcast.82), dimensions={1}, to_apply=%bitcast.120.reduce_sub_computation | reduce | bytes 524290
  47.1 0.8 reshape.108
  47.9 0.8 dynamic_slice.26
  48.6 0.9 %constant_dynamic-slice_fusion.2 = (f32[1,7,256]{2,0,1:T(1,128)S(1)}, f32[1,7,256]{2,0,1:T(1,128)S(1)}) fusion(f32[2,7,1024]{2,0,1:T(2,128)} %param.13, s32[]{:T(128)S(6)} %add.87, s32[]{:T(128)S(6)} %select_n.22), kind=kLoop, calls=%fused_computation.76 | loop fusion | bytes 28680 | tf_op jit(solution)/shard_map/slice | solution.py:144
  49.5 0.7 multiply_exponential_fusion
  50.2 0.4 multiply_reduce_fusion.2
  50.7 0.0 all-to-all-done.1
  50.7 3.4 %all-to-all-start = ((bf16[4,2,16384]{2,1,0:T(2,128)(2,1)}), bf16[4,2,16384]{2,1,0:T(2,128)(2,1)S(1)}, u32[]{:S(2)}, u32[]{:S(2)}) async-start(bf16[4,2,16384]{2,1,0:T(2,128)(2,1)} %reshape.108), calls=%async_computation | async-start | bytes 524288 | tf_op jit(solution)/shard_map/all_to_all | solution.py:175
  54.1 0.3 reshape.107
  54.4 0.1 copy.52
  54.6 0.1 convert_multiply_fusion.3
  54.7 1.3 %collective-permute-start = (f32[6,256]{1,0:T(8,128)S(1)}, f32[6,256]{1,0:T(8,128)S(1)}, u32[]{:S(2)}, u32[]{:S(2)}) collective-permute-start(f32[6,256]{1,0:T(8,128)S(1)} %slice.70), channel_id=1, source_target_pairs={{0,4},{1,5},{2,6},{3,7},{8,12},{9,13},{10,14},{11,15},{16,20},{17,... | collective-permute-start | bytes 18440 | tf_op jit(solution)/shard_map/ppermute | solution.py:29
  56.0 0.0 copy-done
  56.0 0.1 rev.14
  56.1 2.2 %all-to-all-done = bf16[4,2,16384]{2,1,0:T(2,128)(2,1)S(1)} async-done(((bf16[4,2,16384]{2,1,0:T(2,128)(2,1)}), bf16[4,2,16384]{2,1,0:T(2,128)(2,1)S(1)}, u32[]{:S(2)}, u32[]{:S(2)}) %all-to-all-start) | async-done | bytes 262176 | tf_op jit(solution)/shard_map/all_to_all | solution.py:175
  58.3 0.3 reshape.109
  58.6 0.1 copy.50
  58.8 6.3 %collective-permute-done = f32[6,256]{1,0:T(8,128)S(1)} collective-permute-done((f32[6,256]{1,0:T(8,128)S(1)}, f32[6,256]{1,0:T(8,128)S(1)}, u32[]{:S(2)}, u32[]{:S(2)}) %collective-permute-start) | collective-permute-done | bytes 6176 | tf_op jit(solution)/shard_map/ppermute | solution.py:29
  65.1 0.1 reshape.65
  65.3 0.0 copy-start.3
  65.3 0.7 copy-done.3
  66.0 0.1 convolution_select_fusion.1
  66.2 0.1 convert_multiply_fusion.2
  66.3 1.3 %collective-permute-start.1 = (f32[127,256]{1,0:T(8,128)S(1)}, f32[127,256]{1,0:T(8,128)S(1)}, u32[]{:S(2)}, u32[]{:S(2)}) collective-permute-start(f32[127,256]{1,0:T(8,128)S(1)} %slice.75), channel_id=1, source_target_pairs={{0,4},{1,5},{2,6},{3,7},{8,12},{9,13},{10,14},{11,15},{16,20},{17,... | collective-permute-start | bytes 390152 | tf_op jit(solution)/shard_map/ppermute | solution.py:29
  67.6 0.1 rev.15
  67.7 0.1 rev.16
  67.8 0.8 dynamic_slice.33
  68.6 4.8 %all-gather = f32[16,256]{1,0:T(8,128)S(1)} all-gather(f32[8,256]{1,0:T(8,128)S(1)} %get-tuple-element.26), channel_id=2, replica_groups=mesh['sec'=4,'ctx'=2,'ch'=4] {'ctx'}, dimensions={0}, use_global_device_ids=true | all-gather | bytes 24576 | tf_op jit(solution)/shard_map/all_gather | solution.py:14
  73.3 0.0 collective-permute-done.1
  73.4 0.2 broadcast_in_dim.16
  73.5 1.4 %fusion.23 = f32[1,128,256]{2,0,1:T(1,128)S(1)} fusion(f32[1,255,256]{2,0,1:T(1,128)S(1)} %broadcast_in_dim.16, f32[128,1,256]{2,0,1:T(8,128)S(1)} %bitcast.147), kind=kOutput, calls=%fused_computation.46 | convolution fusion | flops 50331648 | bytes 523264 | tf_op jit(solution)/shard_map/conv_general_dilated | solution.py:34
  75.0 0.2 multiply_reduce_fusion.1
  75.3 1.8 %all-gather.1 = f32[16,256]{1,0:T(8,128)S(1)} all-gather(f32[8,256]{1,0:T(8,128)S(1)} %bitcast_add_fusion.1), channel_id=3, replica_groups=mesh['sec'=4,'ctx'=2,'ch'=4] {'ctx'}, dimensions={0}, use_global_device_ids=true | all-gather | bytes 24576 | tf_op jit(solution)/shard_map/all_gather | solution.py:14
  77.1 1.4 %fusion.20 = f32[1,128,256]{2,0,1:T(1,128)S(1)} fusion(f32[128,1,256]{2,0,1:T(8,128)S(1)} %bitcast.146, f32[1,128,256]{2,1,0:T(8,128)S(1)} %get-tuple-element.17), kind=kOutput, calls=%fused_computation.43 | convolution fusion | flops 25362432 | bytes 393216 | tf_op jit(solution)/shard_map/conv_general_dilated | solution.py:34
  78.5 0.5 multiply_reduce_fusion
  79.0 0.1 convert_multiply_fusion
  79.1 1.3 %collective-permute-start.2 = (f32[6,256]{1,0:T(8,128)S(1)}, f32[6,256]{1,0:T(8,128)S(1)}, u32[]{:S(2)}, u32[]{:S(2)}) collective-permute-start(f32[6,256]{1,0:T(8,128)S(1)} %slice.82), channel_id=1, source_target_pairs={{0,4},{1,5},{2,6},{3,7},{8,12},{9,13},{10,14},{11,15},{16,20},{17,... | collective-permute-start | bytes 18440 | tf_op jit(solution)/shard_map/ppermute | solution.py:29
  80.4 0.1 rev.17
  80.5 1.7 %collective-permute-done.2 = f32[6,256]{1,0:T(8,128)S(1)} collective-permute-done((f32[6,256]{1,0:T(8,128)S(1)}, f32[6,256]{1,0:T(8,128)S(1)}, u32[]{:S(2)}, u32[]{:S(2)}) %collective-permute-start.2) | collective-permute-done | bytes 6176 | tf_op jit(solution)/shard_map/ppermute | solution.py:29
  82.2 0.1 reshape.72
  82.4 0.1 convolution_select_fusion
  82.5 0.7 fusion.14
  (27 shorter events, 0.5 us)
Async XLA Ops:
  0.0 56.0 %copy-start = (f32[128,1024]{1,0:T(8,128)S(1)}, f32[128,1024]{1,0:T(8,128)}, u32[]{:S(2)}) copy-start(f32[128,1024]{1,0:T(8,128)} %param.14) | copy-start | bytes 1572868
  4.8 4.4 %copy-start.1 = (bf16[128,256]{1,0:T(8,128)(2,1)S(1)}, bf16[128,256]{1,0:T(8,128)(2,1)}, u32[]{:S(2)}) copy-start(bf16[128,256]{1,0:T(8,128)(2,1)} %param.9) | copy-start | bytes 196612
  4.8 39.7 %copy-start.2 = (bf16[1,128,1024]{2,1,0:T(8,128)(2,1)S(1)}, bf16[1,128,1024]{2,1,0:T(8,128)(2,1)}, u32[]{:S(2)}) copy-start(bf16[1,128,1024]{2,1,0:T(8,128)(2,1)} %param.10) | copy-start | bytes 786436
  4.8 45.8 %all-to-all-start.1 = ((bf16[4,2,16384]{2,1,0:T(2,128)(2,1)}), bf16[4,2,16384]{2,1,0:T(2,128)(2,1)S(1)}, u32[]{:S(2)}, u32[]{:S(2)}) async-start(bf16[4,2,16384]{2,1,0:T(2,128)(2,1)} %reshape.106), calls=%async_computation.1 | async-start | bytes 524288 | tf_op jit(solution)/shard_map/all_to_all | solution.py:176
  50.7 7.6 %all-to-all-start = ((bf16[4,2,16384]{2,1,0:T(2,128)(2,1)}), bf16[4,2,16384]{2,1,0:T(2,128)(2,1)S(1)}, u32[]{:S(2)}, u32[]{:S(2)}) async-start(bf16[4,2,16384]{2,1,0:T(2,128)(2,1)} %reshape.108), calls=%async_computation | async-start | bytes 524288 | tf_op jit(solution)/shard_map/all_to_all | solution.py:175
  54.7 10.4 %collective-permute-start = (f32[6,256]{1,0:T(8,128)S(1)}, f32[6,256]{1,0:T(8,128)S(1)}, u32[]{:S(2)}, u32[]{:S(2)}) collective-permute-start(f32[6,256]{1,0:T(8,128)S(1)} %slice.70), channel_id=1, source_target_pairs={{0,4},{1,5},{2,6},{3,7},{8,12},{9,13},{10,14},{11,15},{16,20},{17,... | collective-permute-start | bytes 18440 | tf_op jit(solution)/shard_map/ppermute | solution.py:29
  65.3 0.7 copy-start.3
  66.3 7.0 %collective-permute-start.1 = (f32[127,256]{1,0:T(8,128)S(1)}, f32[127,256]{1,0:T(8,128)S(1)}, u32[]{:S(2)}, u32[]{:S(2)}) collective-permute-start(f32[127,256]{1,0:T(8,128)S(1)} %slice.75), channel_id=1, source_target_pairs={{0,4},{1,5},{2,6},{3,7},{8,12},{9,13},{10,14},{11,15},{16,20},{17,... | collective-permute-start | bytes 390152 | tf_op jit(solution)/shard_map/ppermute | solution.py:29
  79.1 3.1 %collective-permute-start.2 = (f32[6,256]{1,0:T(8,128)S(1)}, f32[6,256]{1,0:T(8,128)S(1)}, u32[]{:S(2)}, u32[]{:S(2)}) collective-permute-start(f32[6,256]{1,0:T(8,128)S(1)} %slice.82), channel_id=1, source_target_pairs={{0,4},{1,5},{2,6},{3,7},{8,12},{9,13},{10,14},{11,15},{16,20},{17,... | collective-permute-start | bytes 18440 | tf_op jit(solution)/shard_map/ppermute | solution.py:29
where the time goes:
time: 83.9 us; the launch traced here: 83.2 us
  blocking collectives  41.8 us (50%)
  starting transfers between devices  11.7 us (14%)
  waiting for transfers between devices  10.2 us (12%)
  local copies, waits for them, and re-layouts  8.75 us (10%)
  other arithmetic  7.42 us (9%)
  matrix products  2.95 us (4%)
    psum x1, blocking collectives, shards(): summed = lax.psum(squares, ('sec', 'ch'))  35.2 us
    ppermute x3, waiting for transfers between devices, passed_along(): lax.ppermute(value, axis, [(source, source + steps) for source in range(f...  8.03 us
    all_gather x2, blocking collectives, prefix_2(): pieces = jax.tree.map(lambda part: lax.all_gather(part, axis), value)  6.58 us
    unnamed x17, local copies, waits for them, and re-layouts  5.04 us
    unnamed x4, other arithmetic  4.44 us
    all_to_all x1, starting transfers between devices, shards(): lax.all_to_all(key_fields, 'sec', split_axis=2, concat_axis=0, tiled=True)  4.39 us
    ppermute x3, starting transfers between devices, passed_along(): lax.ppermute(value, axis, [(source, source + steps) for source in range(f...  3.88 us
    all_to_all x1, starting transfers between devices, shards(): lax.all_to_all(query_fields, 'sec', split_axis=2, concat_axis=0, tiled=True)  3.42 us
  transfers between devices with their start and end apart: 5, of which 3 were waited for; matrix products, arithmetic and copies ran while one was open for 10% of the time, Pallas kernels for 0%

commit v1 on v0

v1 whole, which is shorter than its diff:
```python
import functools

import jax
import jax.numpy as jnp
from jax import lax
from jax.experimental import pallas as pl
from jax.experimental.pallas import tpu as pltpu
from jax.sharding import PartitionSpec as P

norm_eps = 1e-06
MESH = pl.DeviceIdType.MESH
LANES = 128
ROWS = 8
F32 = jnp.float32


def row_ids(shape):
    return lax.broadcasted_iota(jnp.int32, shape, 0)


def shifted(values, steps):
    if steps == 0:
        return values, jnp.zeros((ROWS, values.shape[1]), F32)
    moved = pltpu.roll(values, steps, 0)
    top = moved[:ROWS]
    inside = row_ids(top.shape) >= steps
    first = jnp.where(inside, top, 0.0)
    if values.shape[0] > ROWS:
        first = jnp.concatenate([first, moved[ROWS:]], axis=0)
    return first, jnp.where(inside, 0.0, top)


def filter_within(values, taps):
    length = values.shape[0]
    span = taps.shape[0]
    total = jnp.zeros(values.shape, F32)
    for step in range(min(ROWS, span)):
        moved, _ = shifted(values, step)
        for tap in range(step, min(span, length), ROWS):
            base = tap - step
            part = moved[: length - base] * taps[tap : tap + 1]
            if base:
                total = jnp.concatenate([total[:base], total[base:] + part], axis=0)
            else:
                total = total + part
    return total


def filter_before(history, taps, length):
    span = taps.shape[0]
    known = history.shape[0]
    total = jnp.zeros((length, history.shape[1]), F32)
    for step in range(min(ROWS, span)):
        moved, fallen = shifted(history, step)
        joined = jnp.concatenate([moved, fallen], axis=0)
        for tap in range(step, span, ROWS):
            base = tap - step
            reach = min(base + ROWS, length)
            part = joined[known - base : known - base + reach] * taps[tap : tap + 1]
            if reach < length:
                total = jnp.concatenate([total[:reach] + part, total[reach:]], axis=0)
            else:
                total = total + part
    return total


def kernel(
    sections,
    n_ctx,
    n_ch,
    inputs,
    query,
    key,
    gain,
    short,
    medium,
    rates,
    residues,
    direct,
    out,
    x_ref,
    gain_ref,
    short_ref,
    medium_ref,
    rate_ref,
    residue_ref,
    direct_ref,
    key_ref,
    query_ref,
    sums_sec,
    sums_ch,
    gated_ref,
    filtered_ref,
    stream_ref,
    tail_ref,
    rows_ref,
    state_ref,
    leaving_ref,
    taps_ref,
    age_ref,
    carry_ref,
    load_sem,
    key_send,
    key_recv,
    query_send,
    query_recv,
    sec_send,
    sec_recv,
    ch_send,
    ch_recv,
    ctx_send,
    ctx_recv,
):
    length, width = x_ref.shape
    modes = rate_ref.shape[0]
    sec = lax.axis_index("sec")
    ctx = lax.axis_index("ctx")
    ch = lax.axis_index("ch")
    has_before = ctx > 0
    has_after = ctx < n_ctx - 1

    def cut(index):
        return pl.ds(pl.multiple_of(index * width, width), width)

    mine = cut(sec)
    loads = [
        pltpu.make_async_copy(inputs, x_ref, load_sem.at[0]),
        pltpu.make_async_copy(rates.at[:, mine], rate_ref, load_sem.at[1]),
        pltpu.make_async_copy(residues.at[:, mine], residue_ref, load_sem.at[2]),
        pltpu.make_async_copy(direct.at[:, mine], direct_ref, load_sem.at[3]),
        pltpu.make_async_copy(gain.at[:, mine], gain_ref, load_sem.at[4]),
        pltpu.make_async_copy(short.at[:, :, mine], short_ref, load_sem.at[5]),
        pltpu.make_async_copy(medium.at[:, mine], medium_ref, load_sem.at[6]),
        pltpu.make_async_copy(key.at[0, :, mine], key_ref.at[sec], key_recv.at[sec]),
        pltpu.make_async_copy(query.at[0, :, mine], query_ref.at[sec], query_recv.at[sec]),
    ]
    for load in loads:
        load.start()

    sec_peers = [lax.rem(sec + step, sections) for step in range(1, sections)]
    ch_peers = [lax.rem(ch + step, n_ch) for step in range(1, n_ch)]
    barrier = pltpu.get_barrier_semaphore()
    for peer in sec_peers:
        pl.semaphore_signal(barrier, inc=1, device_id={"sec": peer}, device_id_type=MESH)
    for peer in ch_peers:
        pl.semaphore_signal(barrier, inc=1, device_id={"ch": peer}, device_id_type=MESH)

    @pl.when(has_before)
    def _():
        pl.semaphore_signal(barrier, inc=1, device_id={"ctx": ctx - 1}, device_id_type=MESH)

    @pl.when(has_after)
    def _():
        pl.semaphore_signal(barrier, inc=1, device_id={"ctx": ctx + 1}, device_id_type=MESH)

    loads[0].wait()
    squares = jnp.square(x_ref[...].astype(F32))
    folded = sum(squares[:, low : low + LANES] for low in range(0, width, LANES))
    partial = jnp.sum(folded.T, axis=0, keepdims=True)
    sums_sec[sec] = jnp.broadcast_to(partial, sums_sec.shape[1:])

    around = has_before.astype(jnp.int32) + has_after.astype(jnp.int32)
    pl.semaphore_wait(barrier, len(sec_peers) + len(ch_peers) + around)

    def remote(src, dst, send_sem, recv_sem, device):
        return pltpu.make_async_remote_copy(
            src_ref=src,
            dst_ref=dst,
            send_sem=send_sem,
            recv_sem=recv_sem,
            device_id=device,
            device_id_type=MESH,
        )

    sends = []
    for step, peer in enumerate(sec_peers):
        slot = sums_sec.at[sec]
        sends.append(remote(slot, slot, sec_send.at[step], sec_recv.at[sec], {"sec": peer}))
    for field, held, send_sem, recv_sem in (
        (key, key_ref, key_send, key_recv),
        (query, query_ref, query_send, query_recv),
    ):
        for step, peer in enumerate(sec_peers):
            sends.append(
                remote(
                    field.at[0, :, cut(peer)],
                    held.at[sec],
                    send_sem.at[step],
                    recv_sem.at[sec],
                    {"sec": peer},
                )
            )
    for send in sends:
        send.start()

    def arrived(ref, sem):
        pltpu.make_async_copy(ref, ref, sem).wait()

    for load in loads[1:4]:
        load.wait()
    offsets = row_ids((length, width)).astype(F32)
    rate_table = rate_ref[...]
    weights = residue_ref[...] * jnp.sqrt(1.0 - jnp.exp(-2.0 * rate_table))
    taps = jnp.where(row_ids((length, width)) == 0, direct_ref[...], 0.0)
    for mode in range(modes):
        part = weights[mode : mode + 1] * jnp.exp(-rate_table[mode : mode + 1] * offsets)
        carry_ref[mode] = part
        taps = taps + part
    taps_ref[...] = taps

    for peer in sec_peers:
        arrived(sums_sec.at[peer], sec_recv.at[peer])
    total = sums_sec[0]
    for index in range(1, sections):
        total = total + sums_sec[index]
    sums_ch[ch] = total
    for step, peer in enumerate(ch_peers):
        slot = sums_ch.at[ch]
        send = remote(slot, slot, ch_send.at[step], ch_recv.at[ch], {"ch": peer})
        send.start()
        sends.append(send)

    @pl.when(has_after)
    def _():
        ages = (length - 1.0) - offsets
        for mode in range(modes):
            age_ref[mode] = jnp.exp(-rate_table[mode : mode + 1] * ages)

    for load in loads[4:7]:
        load.wait()

    for peer in ch_peers:
        arrived(sums_ch.at[peer], ch_recv.at[peer])
    total = sums_ch[0]
    for index in range(1, n_ch):
        total = total + sums_ch[index]
    inverse = lax.rsqrt(total / (width * sections * n_ch) + norm_eps)
    scale = jnp.broadcast_to(inverse[:1], (length, length)).T[:, :1]
    stream = x_ref[...].astype(F32) * scale * gain_ref[...]
    stream_ref[...] = stream.astype(jnp.bfloat16).astype(F32)

    halves = [slice(low, low + LANES) for low in range(0, width, LANES)]
    after = {"ctx": lax.rem(ctx + 1, n_ctx)}

    def short_section(section, tap_set, tail_slot):
        hand = remote(
            gated_ref.at[section, pl.ds(length - ROWS, ROWS)],
            tail_ref.at[tail_slot],
            ctx_send.at[section],
            ctx_recv.at[section],
            after,
        )

        @pl.when(has_after)
        def _():
            hand.start()

        for half in halves:
            filtered_ref[:, half] = filter_within(
                gated_ref[section, :, half], short_ref[tap_set, :, half]
            )

        @pl.when(has_before)
        def _():
            hand.wait_recv()
            for half in halves:
                filtered_ref[:ROWS, half] += filter_before(
                    tail_ref[tail_slot, :, half], short_ref[tap_set, :, half], ROWS
                )

        return hand

    def medium_section(section):
        hand = remote(
            gated_ref.at[section], rows_ref, ctx_send.at[section], ctx_recv.at[section], after
        )

        @pl.when(has_after)
        def _():
            hand.start()

        for half in halves:
            filtered_ref[:, half] = filter_within(
                gated_ref[section, :, half], medium_ref[:, half]
            )

        @pl.when(has_before)
        def _():
            hand.wait_recv()
            for half in halves:
                filtered_ref[:, half] += filter_before(
                    rows_ref[:, half], medium_ref[:, half], length
                )

        return hand

    def long_section(section):
        hand = remote(leaving_ref, state_ref, ctx_send.at[section], ctx_recv.at[section], after)

        @pl.when(has_after)
        def _():
            for mode in range(modes):
                leaving_ref[mode : mode + 1] = jnp.sum(
                    age_ref[mode] * gated_ref[section], axis=0, keepdims=True
                )

        @pl.when(jnp.logical_and(has_after, jnp.logical_not(has_before)))
        def _():
            hand.start()

        @pl.when(has_before)
        def _():
            hand.wait_recv()

        @pl.when(jnp.logical_and(has_after, has_before))
        def _():
            leaving_ref[...] += jnp.exp(-length * rate_ref[...]) * state_ref[...]
            hand.start()

        for half in halves:
            filtered_ref[:, half] = filter_within(gated_ref[section, :, half], taps_ref[:, half])

        @pl.when(has_before)
        def _():
            entering = jnp.exp(-rate_ref[...]) * state_ref[...]
            for half in halves:
                carried = filtered_ref[:, half]
                for mode in range(modes):
                    carried = carried + carry_ref[mode, :, half] * entering[mode : mode + 1, half]
                filtered_ref[:, half] = carried

        return hand

    hands = []
    for section in range(sections):
        arrived(key_ref.at[section], key_recv.at[section])
        gated_ref[section] = key_ref[section].astype(F32) * stream_ref[...]
        if section == 1:
            hands.append(medium_section(section))
        elif section == 2:
            hands.append(long_section(section))
        else:
            hands.append(short_section(section, min(section, 1), min(section, 1)))
        arrived(query_ref.at[section], query_recv.at[section])
        stream = stream_ref[...] + query_ref[section].astype(F32) * filtered_ref[...]
        if section == sections - 1:
            out[...] = stream.astype(jnp.bfloat16)
        else:
            stream_ref[...] = stream.astype(jnp.bfloat16).astype(F32)

    for send in sends:
        send.wait_send()

    @pl.when(has_after)
    def _():
        for hand in hands:
            hand.wait_send()


def shards(
    inputs,
    query_fields,
    key_fields,
    norm_gain,
    short_taps,
    medium_taps,
    pole_rates,
    pole_residues,
    direct_term,
):
    sections = lax.axis_size("sec")
    n_ctx = lax.axis_size("ctx")
    n_ch = lax.axis_size("ch")
    length, width = inputs.shape
    modes = pole_rates.shape[0]
    shorts, short_span = short_taps.shape[:2]
    anywhere = pl.BlockSpec(memory_space=pl.ANY)
    dma = pltpu.SemaphoreType.DMA
    return pl.pallas_call(
        functools.partial(kernel, sections, n_ctx, n_ch),
        out_shape=jax.ShapeDtypeStruct((length, width), inputs.dtype),
        in_specs=[anywhere] * 9,
        out_specs=pl.BlockSpec(memory_space=pltpu.VMEM),
        scratch_shapes=[
            pltpu.VMEM((length, width), inputs.dtype),
            pltpu.VMEM((1, width), F32),
            pltpu.VMEM((shorts, short_span, width), F32),
            pltpu.VMEM((medium_taps.shape[0], width), F32),
            pltpu.VMEM((modes, width), F32),
            pltpu.VMEM((modes, width), F32),
            pltpu.VMEM((1, width), F32),
            pltpu.VMEM((sections, length, width), key_fields.dtype),
            pltpu.VMEM((sections, length, width), query_fields.dtype),
            pltpu.VMEM((sections, ROWS, length), F32),
            pltpu.VMEM((n_ch, ROWS, length), F32),
            pltpu.VMEM((sections, length, width), F32),
            pltpu.VMEM((length, width), F32),
            pltpu.VMEM((length, width), F32),
            pltpu.VMEM((2, ROWS, width), F32),
            pltpu.VMEM((length, width), F32),
            pltpu.VMEM((modes, width), F32),
            pltpu.VMEM((modes, width), F32),
            pltpu.VMEM((length, width), F32),
            pltpu.VMEM((modes, length, width), F32),
            pltpu.VMEM((modes, length, width), F32),
            dma((7,)),
            dma((sections - 1,)),
            dma((sections,)),
            dma((sections - 1,)),
            dma((sections,)),
            dma((sections - 1,)),
            dma((sections,)),
            dma((n_ch - 1,)),
            dma((n_ch,)),
            dma((sections,)),
            dma((sections,)),
        ],
        compiler_params=pltpu.CompilerParams(collective_id=0, has_side_effects=True),
    )(
        inputs,
        query_fields,
        key_fields,
        norm_gain[None],
        short_taps,
        medium_taps,
        pole_rates,
        pole_residues,
        direct_term[None],
    )


def solution(mesh):
    in_specs = (
        P("ctx", ("ch", "sec")),
        P("sec", "ctx", "ch"),
        P("sec", "ctx", "ch"),
        P("ch"),
        P(None, None, "ch"),
        P(None, "ch"),
        P(None, "ch"),
        P(None, "ch"),
        P("ch"),
    )
    out_specs = P("ctx", ("ch", "sec"))
    return jax.shard_map(shards, mesh=mesh, in_specs=in_specs, out_specs=out_specs, check_vma=False)
```

time: 83.9 us -> 19.7 us (0.23)
  blocking collectives: 41.8 us -> 0 us
  Pallas kernels: 0 us -> 16.5 us
  starting transfers between devices: 11.7 us -> 0 us
  waiting for transfers between devices: 10.2 us -> 0 us
  other arithmetic: 7.42 us -> 0 us
  local copies, waits for them, and re-layouts: 8.75 us -> 2.94 us
  matrix products: 2.95 us -> 0 us
    psum x1 -> x0, blocking collectives: 35.2 us -> none  [shards(): summed = lax.psum(squares, ('sec', 'ch'))]
    pallas_call x0 -> x1, Pallas kernels: none -> 16.5 us  [shards(): pl.pallas_call(functools.partial(kernel, sections, n_ctx, n_ch), out_shap...]
    ppermute x3 -> x0, waiting for transfers between devices: 8.03 us -> none  [passed_along(): lax.ppermute(value, axis, [(source, source + steps) for source in range(f...]
    all_to_all x2 -> x0, starting transfers between devices: 7.8 us -> none  [the longest x1 4.39 us: shards(): lax.all_to_all(key_fields, 'sec', split_axis=2, concat_axis=0, tiled=True)]
    all_gather x2 -> x0, blocking collectives: 6.58 us -> none  [prefix_2(): pieces = jax.tree.map(lambda part: lax.all_gather(part, axis), value)]
    unnamed x4 -> x0, other arithmetic: 4.44 us -> none
    ppermute x3 -> x0, starting transfers between devices: 3.88 us -> none  [passed_along(): lax.ppermute(value, axis, [(source, source + steps) for source in range(f...]
    conv_general_dilated x4 -> x0, matrix products: 2.95 us -> none  [batched_depthwise(): lax.conv_general_dilated(padded, flipped_taps[:, None, :], window_strides...]
  transfers between devices with their start and end apart: 5 -> 0, of which waited for: 3 -> 0; matrix products, arithmetic and copies ran while one was open for 10% -> 0% of each run, Pallas kernels for 0% -> 0%
where the time goes in v1:
time: 19.7 us; the launch traced here: 19.4 us
  Pallas kernels  16.5 us (84%)
  local copies, waits for them, and re-layouts  2.94 us (15%)
    pallas_call x1, Pallas kernels, shards(): pl.pallas_call(functools.partial(kernel, sections, n_ctx, n_ch), out_shap...  16.5 us
    unnamed x2, local copies, waits for them, and re-layouts  2.94 us

profile of v1, /device:TPU:1, one launch (start us, length us, event | category | flops | bytes accessed | tf_op | source)
XLA Modules:
  0.0 19.4 jit_solution(7408871837536644678)
XLA Ops:
  0.0 1.5 %copy.10.short = f32[2,7,1024]{2,1,0:T(8,128)} copy(f32[2,7,1024]{2,0,1:T(2,128)} %param.13) | data formatting | bytes 114688 | tf_op args[4]
  1.5 16.5 %shard_map.91 = bf16[128,256]{1,0:T(8,128)(2,1)} custom-call(bf16[128,256]{1,0:T(8,128)(2,1)} %inputs.1, bf16[1,128,1024]{2,1,0:T(8,128)(2,1)} %query.1, bf16[1,128,1024]{2,1,0:T(8,128)(2,1)} %key.1, f32[1,1024]{1,0:T(1,128)} %bitcast.2, f32[2,7,1024]{2,1,0:T(8,128)} %copy.10.short, f32[128,1024]{1,0:T(8,128)} %medium.1, f32[8,1024]{1,0:T(8,128)} %rates.1, ...), custom_call_target="tpu_custom_call" | custom-call | tf_op jit(solution)/shard_map/pallas_call | solution.py:379
  18.0 1.5 %copy.12 = bf16[128,256]{1,0:T(8,128)(2,1)} copy(bf16[128,256]{1,0:T(8,128)(2,1)} %shard_map.91) | data formatting | bytes 131072

commit v2 on v1

--- a/solution.py
+++ b/solution.py
@@ -46,16 +46,16 @@
     return total
 
 
-def filter_before(history, taps, length):
+def filter_before(history, taps, length, own=0):
     span = taps.shape[0]
-    known = history.shape[0]
+    known = history.shape[0] - own
     total = jnp.zeros((length, history.shape[1]), F32)
     for step in range(min(ROWS, span)):
         moved, fallen = shifted(history, step)
         joined = jnp.concatenate([moved, fallen], axis=0)
         for tap in range(step, span, ROWS):
             base = tap - step
-            reach = min(base + ROWS, length)
+            reach = min(base + ROWS + own, length)
             part = joined[known - base : known - base + reach] * taps[tap : tap + 1]
             if reach < length:
                 total = jnp.concatenate([total[:reach] + part, total[reach:]], axis=0)
@@ -99,6 +99,7 @@
     taps_ref,
     age_ref,
     carry_ref,
+    top_ref,
     load_sem,
     key_send,
     key_recv,
@@ -157,7 +158,7 @@
     squares = jnp.square(x_ref[...].astype(F32))
     folded = sum(squares[:, low : low + LANES] for low in range(0, width, LANES))
     partial = jnp.sum(folded.T, axis=0, keepdims=True)
-    sums_sec[sec] = jnp.broadcast_to(partial, sums_sec.shape[1:])
+    sums_sec[sec] = partial
 
     around = has_before.astype(jnp.int32) + has_after.astype(jnp.int32)
     pl.semaphore_wait(barrier, len(sec_peers) + len(ch_peers) + around)
@@ -257,25 +258,34 @@
 
         for half in halves:
             filtered_ref[:, half] = filter_within(
-                gated_ref[section, :, half], short_ref[tap_set, :, half]
+                gated_ref[section, :, half], short_ref[:, tap_set, half]
             )
 
+        if section:
+
+            @pl.when(has_before)
+            def _():
+                hand.wait_recv()
+                finish_top(tail_slot, tap_set)
+
+        return hand
+
+    def finish_top(tail_slot, tap_set):
+        for half in halves:
+            filtered_ref[:ROWS, half] += filter_before(
+                tail_ref[tail_slot, :, half], short_ref[:, tap_set, half], ROWS
+            )
+
+    def medium_section(section, earlier):
         @pl.when(has_before)
         def _():
-            hand.wait_recv()
-            for half in halves:
-                filtered_ref[:ROWS, half] += filter_before(
-                    tail_ref[tail_slot, :, half], short_ref[tap_set, :, half], ROWS
-                )
-
-        return hand
-
-    def medium_section(section):
+            gated_ref[section, :ROWS] = jnp.zeros((ROWS, width), F32)
+
         hand = remote(
             gated_ref.at[section], rows_ref, ctx_send.at[section], ctx_recv.at[section], after
         )
 
-        @pl.when(has_after)
+        @pl.when(jnp.logical_and(has_after, jnp.logical_not(has_before)))
         def _():
             hand.start()
 
@@ -286,10 +296,28 @@
 
         @pl.when(has_before)
         def _():
+            earlier.wait_recv()
+            for half in halves:
+                added = filter_before(tail_ref[0, :, half], short_ref[:, 0, half], ROWS)
+                gate = query_ref[section - 1, :ROWS, half].astype(F32)
+                top = top_ref[0, :, half] + gate * (top_ref[1, :, half] + added)
+                top = top.astype(jnp.bfloat16).astype(F32)
+                stream_ref[:ROWS, half] = top
+                gated_ref[section, :ROWS, half] = key_ref[section, :ROWS, half].astype(F32) * top
+
+        @pl.when(jnp.logical_and(has_after, has_before))
+        def _():
+            hand.start()
+
+        @pl.when(has_before)
+        def _():
             hand.wait_recv()
             for half in halves:
+                history = jnp.concatenate(
+                    [rows_ref[:, half], gated_ref[section, :ROWS, half]], axis=0
+                )
                 filtered_ref[:, half] += filter_before(
-                    rows_ref[:, half], medium_ref[:, half], length
+                    history, medium_ref[:, half], length, ROWS
                 )
 
         return hand
@@ -336,12 +364,15 @@
         arrived(key_ref.at[section], key_recv.at[section])
         gated_ref[section] = key_ref[section].astype(F32) * stream_ref[...]
         if section == 1:
-            hands.append(medium_section(section))
+            hands.append(medium_section(section, hands[0]))
         elif section == 2:
             hands.append(long_section(section))
         else:
             hands.append(short_section(section, min(section, 1), min(section, 1)))
         arrived(query_ref.at[section], query_recv.at[section])
+        if section == 0:
+            top_ref[0] = stream_ref[:ROWS]
+            top_ref[1] = filtered_ref[:ROWS]
         stream = stream_ref[...] + query_ref[section].astype(F32) * filtered_ref[...]
         if section == sections - 1:
             out[...] = stream.astype(jnp.bfloat16)
@@ -374,6 +405,7 @@
     length, width = inputs.shape
     modes = pole_rates.shape[0]
     shorts, short_span = short_taps.shape[:2]
+    hbm = pl.BlockSpec(memory_space=pltpu.HBM)
     anywhere = pl.BlockSpec(memory_space=pl.ANY)
     dma = pltpu.SemaphoreType.DMA
     return pl.pallas_call(
@@ -384,15 +416,15 @@
         scratch_shapes=[
             pltpu.VMEM((length, width), inputs.dtype),
             pltpu.VMEM((1, width), F32),
-            pltpu.VMEM((shorts, short_span, width), F32),
+            pltpu.VMEM((short_span, shorts, width), F32),
             pltpu.VMEM((medium_taps.shape[0], width), F32),
             pltpu.VMEM((modes, width), F32),
             pltpu.VMEM((modes, width), F32),
             pltpu.VMEM((1, width), F32),
             pltpu.VMEM((sections, length, width), key_fields.dtype),
             pltpu.VMEM((sections, length, width), query_fields.dtype),
-            pltpu.VMEM((sections, ROWS, length), F32),
-            pltpu.VMEM((n_ch, ROWS, length), F32),
+            pltpu.VMEM((sections, 1, length), F32),
+            pltpu.VMEM((n_ch, 1, length), F32),
             pltpu.VMEM((sections, length, width), F32),
             pltpu.VMEM((length, width), F32),
             pltpu.VMEM((length, width), F32),
@@ -403,6 +435,7 @@
             pltpu.VMEM((length, width), F32),
             pltpu.VMEM((modes, length, width), F32),
             pltpu.VMEM((modes, length, width), F32),
+            pltpu.VMEM((2, ROWS, width), F32),
             dma((7,)),
             dma((sections - 1,)),
             dma((sections,)),
@@ -421,7 +454,7 @@
         query_fields,
         key_fields,
         norm_gain[None],
-        short_taps,
+        jnp.swapaxes(short_taps, 0, 1),
         medium_taps,
         pole_rates,
         pole_residues,

time: 19.7 us -> 17.6 us (0.89)
  local copies, waits for them, and re-layouts: 2.94 us -> 1.47 us
  Pallas kernels: 16.5 us -> 15.9 us
    unnamed x2 -> x1, local copies, waits for them, and re-layouts: 2.94 us -> 1.47 us
    pallas_call x1, Pallas kernels: 16.5 us -> 15.9 us  [shards(): pl.pallas_call(functools.partial(kernel, sections, n_ctx, n_ch), out_shap...]
where the time goes in v2:
time: 17.6 us; the launch traced here: 17.4 us
  Pallas kernels  15.9 us (90%)
  local copies, waits for them, and re-layouts  1.47 us (8%)
    pallas_call x1, Pallas kernels, shards(): pl.pallas_call(functools.partial(kernel, sections, n_ctx, n_ch), out_shap...  15.9 us
    unnamed x1, local copies, waits for them, and re-layouts  1.47 us

profile of v2, /device:TPU:1, one launch (start us, length us, event | category | flops | bytes accessed | tf_op | source)
XLA Modules:
  0.0 17.4 jit_solution(1531899416527225132)
XLA Ops:
  0.0 15.9 %shard_map.91 = bf16[128,256]{1,0:T(8,128)(2,1)} custom-call(bf16[128,256]{1,0:T(8,128)(2,1)} %inputs.1, bf16[1,128,1024]{2,1,0:T(8,128)(2,1)} %query.1, bf16[1,128,1024]{2,1,0:T(8,128)(2,1)} %key.1, f32[1,1024]{1,0:T(1,128)} %bitcast.4, f32[7,2,1024]{2,1,0:T(2,128)} %bitcast.3, f32[128,1024]{1,0:T(8,128)} %medium.1, f32[8,1024]{1,0:T(8,128)} %rates.1, ...), custom_call_target="tpu_custom_call" | custom-call | tf_op jit(solution)/shard_map/pallas_call | solution.py:411
  15.9 1.5 %copy.11 = bf16[128,256]{1,0:T(8,128)(2,1)} copy(bf16[128,256]{1,0:T(8,128)(2,1)} %shard_map.91) | data formatting | bytes 131072
